TPU v7x, 128 devices: a whole 4x4x4 slice. The times are simulated.
128 devices in a mesh: ingest: 4 (over x), owner: 32 (over y, z, core).
Axes of the slice: x: 4, y: 4, z: 4, core: 2. Of those that a mesh axis runs over, the one named last changes fastest.
Arguments:
- frame_mel: bfloat16 [131072, 48], P(('ingest', 'owner')), may hold values from -6 to 6
- row_device: int32 [131072, 1], P(('ingest', 'owner')), may hold values from 0 to 127; in each aligned block of 1024 rows (0 to 1023, 1024 to 2047, ...) at most 11 rows name the same one
- row_slot: int32 [131072], P(('ingest', 'owner')), may hold values from 0 to 3
- window_length: int32 [512], replicated, may hold values from 2 to 512, as said below
- migrate_count: int32 [128], replicated, may hold values from 0 to 2, as said below
- conv_state: bfloat16 [512, 256], P(('ingest', 'owner')), may hold values from -6 to 6
- kv_cache: bfloat16 [512, 2, 512, 256], P(('ingest', 'owner'))
- w_in: bfloat16 [48, 256], replicated, may hold values from -0.875 to 0.875
- w_state: bfloat16 [256, 256], replicated, may hold values from -0.375 to 0.375
- w_qkv: bfloat16 [256, 768], replicated, may hold values from -0.375 to 0.375
- w_out: bfloat16 [256, 256], replicated, may hold values from -0.375 to 0.375
Outputs:
- frame_scores: bfloat16 [131072, 256], P(('ingest', 'owner'))
- new_state: bfloat16 [768, 256], P(('ingest', 'owner'))
Inputs may be any that keep to these rules, and one draw needn't show every extreme that they name: `row_device`: no device is named by more than 11 rows of one device; some device reaches it. `window_length`: the first session of every device has 512 valid frames. `migrate_count`: a device's migrated sessions are its highest slots; some device moves 2.
All inputs are finite; a program needn't handle non-finite values.
Results may differ from a plain program's by a relative error of at most 0.0087.
Values may be sent and summed in bfloat16 or wider, within the bound.
A program may use at most 64 MiB of HBM per device.

v0:
```python
import jax
import jax.numpy as jnp
from jax import lax
from jax.sharding import PartitionSpec as P

HEADS = 4
MIG = 2


def from_behind(shard, axis, by):
    length = lax.axis_size(axis)
    return lax.ppermute(shard, axis, [(i, (i + by) % length) for i in range(length)])


def pack_rows(feats, target, labels, devices, depth):
    match = (target[:, None] == jnp.arange(devices, dtype=jnp.int32)[None, :]).astype(jnp.int32)
    ranks = jnp.sum(jnp.cumsum(match, axis=0) * match, axis=1) - 1
    spots = target * depth + ranks
    picker = spots[:, None] == jnp.arange(devices * depth, dtype=jnp.int32)[None, :]
    buffer = jnp.einsum(
        "rb,rc->bc", picker.astype(feats.dtype), feats, preferred_element_type=jnp.float32
    ).astype(feats.dtype)
    slot_ids = jnp.sum(picker.astype(jnp.int32) * (labels[:, None] + 1), axis=0) - 1
    return (buffer, slot_ids, picker)


def send_rows(buffer, slot_ids, n_ing, n_own, depth):
    width = buffer.shape[1]
    got_rows, got_slots = (
        lax.all_to_all(
            buffer.reshape(n_ing * n_own, depth, width),
            ("ingest", "owner"),
            split_axis=0,
            concat_axis=0,
            tiled=True,
        ),
        lax.all_to_all(
            slot_ids.reshape(n_ing * n_own, depth),
            ("ingest", "owner"),
            split_axis=0,
            concat_axis=0,
            tiled=True,
        ),
    )
    return (got_rows.reshape(-1, width), got_slots.reshape(-1))


def send_back(scored, n_ing, n_own, depth):
    width = scored.shape[1]
    returned = lax.all_to_all(
        scored.reshape(n_ing * n_own, depth, width),
        ("ingest", "owner"),
        split_axis=0,
        concat_axis=0,
        tiled=True,
    )
    return returned.reshape(-1, width)


def score_rows(inputs, slot_ids, states, cache, lengths, w_state, w_qkv, w_out):
    rows, width = inputs.shape
    slots = states.shape[0]
    window = cache.shape[2]
    head_dim = width // HEADS
    scale = head_dim ** (-0.5)
    block = 64
    carried = jnp.dot(states, w_state, preferred_element_type=jnp.float32)
    picker = (slot_ids[:, None] == jnp.arange(slots, dtype=jnp.int32)[None, :]).astype(jnp.float32)
    chosen = jnp.dot(picker, carried, precision=lax.Precision.HIGHEST)
    hidden = jax.nn.silu(inputs.astype(jnp.float32) + chosen).astype(jnp.bfloat16)
    qkv = jnp.dot(hidden, w_qkv, preferred_element_type=jnp.float32).astype(jnp.bfloat16)
    match = picker.astype(jnp.int32)
    present = jnp.sum(match, axis=1) > 0
    slot_counts = jnp.sum(match, axis=0)
    ranks = jnp.sum(jnp.cumsum(match, axis=0) * match, axis=1) - 1
    spans = (slot_counts + block - 1) // block
    block_ends = jnp.cumsum(spans)
    block_starts = block_ends - spans
    block_total = (rows + block - 1) // block + slots
    row_block = jnp.sum(match * block_starts[None, :], axis=1)
    place = jnp.where(present, row_block * block + ranks, block_total * block)
    padded = (
        jnp.zeros((block_total * block, 3 * width), jnp.bfloat16).at[place].set(qkv, mode="drop")
    )
    block_ids = jnp.arange(block_total, dtype=jnp.int32)
    block_slot = jnp.sum((block_ends[None, :] <= block_ids[:, None]).astype(jnp.int32), axis=1)
    block_slot = jnp.minimum(block_slot, slots - 1)
    positions = jnp.arange(window, dtype=jnp.int32)

    def per_block(index):
        taken = lax.dynamic_slice_in_dim(padded, index * block, block, 0)
        which = block_slot[index]
        part = lax.dynamic_index_in_dim(cache, which, 0, keepdims=False)
        keys = part[0].reshape(window, HEADS, head_dim)
        values = part[1].reshape(window, HEADS, head_dim)
        valid = positions < lengths[which]
        group_q = taken[:, :width].reshape(block, HEADS, head_dim)
        group_k = taken[:, width : 2 * width].reshape(block, HEADS, head_dim)
        group_v = taken[:, 2 * width :].reshape(block, HEADS, head_dim)
        own = (
            jnp.einsum("rhd,rhd->hr", group_q, group_k, preferred_element_type=jnp.float32) * scale
        )
        score = (
            jnp.einsum("rhd,phd->hrp", group_q, keys, preferred_element_type=jnp.float32) * scale
        )
        score = jnp.where(valid[None, None, :], score, -1e30)
        top = jnp.maximum(jnp.max(score, axis=-1), own)
        expo = jnp.exp(score - top[..., None])
        own_exp = jnp.exp(own - top)
        total = jnp.sum(expo, axis=-1) + own_exp
        weights = (expo / total[..., None]).astype(jnp.bfloat16)
        own_weight = (own_exp / total).astype(jnp.bfloat16)
        mixed = jnp.einsum("hrp,phd->rhd", weights, values, preferred_element_type=jnp.float32)
        mixed = mixed + own_weight.astype(jnp.float32).T[:, :, None] * group_v.astype(jnp.float32)
        return mixed.reshape(block, width).astype(jnp.bfloat16)

    blocks_out = lax.map(per_block, block_ids).reshape(block_total * block, width)
    fetched = blocks_out[jnp.minimum(place, block_total * block - 1)]
    attn = jnp.where(present[:, None], fetched, jnp.zeros_like(fetched))
    scored = (
        hidden.astype(jnp.float32) + jnp.dot(attn, w_out, preferred_element_type=jnp.float32)
    ).astype(jnp.bfloat16)
    sums = jnp.dot(picker.T, scored.astype(jnp.float32), precision=lax.Precision.HIGHEST)
    counts = jnp.sum(picker, axis=0)
    mean = sums / jnp.maximum(counts, 1.0)[:, None]
    updated = jnp.where(counts[:, None] > 0, mean, states.astype(jnp.float32)).astype(jnp.bfloat16)
    return (scored, updated)


def body(
    frame_mel,
    row_device,
    row_slot,
    window_length,
    migrate_count,
    conv_state,
    kv_cache,
    w_in,
    w_state,
    w_qkv,
    w_out,
):
    n_ing = lax.axis_size("ingest")
    n_own = lax.axis_size("owner")
    devices = n_ing * n_own
    rows_dev = frame_mel.shape[0]
    sessions = conv_state.shape[0]
    capacity = max(2, 11 * rows_dev // (8 * devices))
    owner_index = lax.axis_index("owner")
    here = lax.axis_index("ingest") * n_own + owner_index
    before = lax.axis_index("ingest") * n_own + (owner_index + n_own - 1) % n_own
    feats = jnp.dot(frame_mel, w_in, preferred_element_type=jnp.float32).astype(jnp.bfloat16)
    target = row_device[:, 0]
    own_lengths = lax.dynamic_slice_in_dim(window_length, here * sessions, sessions)
    depth = 2 * capacity
    following = target // n_own * n_own + (target % n_own + 1) % n_own
    leaving = row_slot >= sessions - migrate_count[target]
    dest = jnp.where(leaving, following, target)
    labels = jnp.where(leaving, row_slot + MIG, row_slot)
    moved_states, moved_cache = from_behind(
        (conv_state[sessions - MIG :], kv_cache[sessions - MIG :]), "owner", 1
    )
    states = jnp.concatenate([conv_state, moved_states], axis=0)
    cache = jnp.concatenate([kv_cache, moved_cache], axis=0)
    in_lengths = lax.dynamic_slice_in_dim(window_length, before * sessions + sessions - MIG, MIG)
    lengths = jnp.concatenate([own_lengths, in_lengths], axis=0)
    buffer, slot_ids, picker = pack_rows(feats, dest, labels, devices, depth)
    got_rows, got_slots = send_rows(buffer, slot_ids, n_ing, n_own, depth)
    scored, updated = score_rows(got_rows, got_slots, states, cache, lengths, w_state, w_qkv, w_out)
    returned = send_back(scored, n_ing, n_own, depth)
    frame_scores = jnp.dot(
        picker.astype(returned.dtype), returned, preferred_element_type=jnp.float32
    ).astype(jnp.bfloat16)
    keep_own = jnp.arange(sessions, dtype=jnp.int32) < sessions - migrate_count[here]
    live_in = jnp.arange(MIG, dtype=jnp.int32) >= MIG - migrate_count[before]
    own_part = jnp.where(keep_own[:, None], updated[:sessions], jnp.zeros_like(updated[:sessions]))
    in_part = jnp.where(live_in[:, None], updated[sessions:], jnp.zeros_like(updated[sessions:]))
    new_state = jnp.concatenate([own_part, in_part], axis=0)
    return (frame_scores, new_state)


def solution(mesh):
    placed = (
        P(("ingest", "owner"), None),
        P(("ingest", "owner"), None),
        P(("ingest", "owner")),
        P(),
        P(),
        P(("ingest", "owner"), None),
        P(("ingest", "owner"), None, None, None),
        P(),
        P(),
        P(),
        P(),
    )
    return jax.shard_map(
        body,
        mesh=mesh,
        in_specs=placed,
        out_specs=(P(("ingest", "owner"), None), P(("ingest", "owner"), None)),
        check_vma=False,
    )
```

profile of v0, /device:TPU:1, one launch (start us, length us, event | category | flops | bytes accessed | tf_op | source)
XLA Modules:
  0.0 649.3 jit_solution(3294324548985979866)
XLA Ops:
  1.4 6.6 %gather_fusion = s32[1024]{0:T(1024)S(1)} fusion(s32[128]{0:T(128)S(1)} %copy-done.1, s32[1024]{0:T(1024)S(1)} %broadcast_clamp_fusion), kind=kCustom, calls=%fused_computation | custom fusion | bytes 12288 | tf_op jit(solution)/shard_map/gather | solution.py:157
  9.0 4.1 select_reduce_fusion
  13.8 11.5 %all-to-all-start.1 = ((s32[128,1,22]{2,1,0:T(1,128)}), s32[128,1,22]{2,1,0:T(1,128)S(1)}, u32[]{:S(2)}, u32[]{:S(2)}) async-start(s32[128,1,22]{2,1,0:T(1,128)} %bitcast.8), calls=%async_computation.1 | async-start | bytes 131072 | tf_op jit(solution)/shard_map/all_to_all | solution.py:37
  25.4 1.8 collective-permute-start
  27.2 4.1 copy.37
  31.4 2.3 slice.60
  35.8 3.4 fusion.16
  39.8 1.3 reshape.285
  42.8 9.8 %all-to-all-start = ((bf16[128,22,256]{2,1,0:T(8,128)(2,1)}), bf16[128,22,256]{2,1,0:T(8,128)(2,1)}, u32[]{:S(2)}, u32[]{:S(2)}) async-start(bf16[128,22,256]{2,1,0:T(8,128)(2,1)} %reshape.285), calls=%async_computation | async-start | bytes 3145728 | tf_op jit(solution)/shard_map/all_to_all | solution.py:30
  54.6 1.7 reduce-window.30
  57.2 3.8 pad_maximum_fusion
  61.0 16.2 %all-to-all-done = bf16[128,22,256]{2,1,0:T(8,128)(2,1)} async-done(((bf16[128,22,256]{2,1,0:T(8,128)(2,1)}), bf16[128,22,256]{2,1,0:T(8,128)(2,1)}, u32[]{:S(2)}, u32[]{:S(2)}) %all-to-all-start) | async-done | bytes 1441824 | tf_op jit(solution)/shard_map/all_to_all | solution.py:30
  77.3 3.5 reshape.292
  80.7 3.5 multiply_convert_fusion
  84.3 3.3 convolution_convert_fusion
  87.6 19.0 %scatter_custom_fusion = bf16[3200,768]{1,0:T(8,128)(2,1)} fusion(s32[2816]{0:T(1024)S(1)} %get-tuple-element.62, bf16[2816,768]{1,0:T(8,128)(2,1)} %convolution_convert_fusion, bf16[]{:T(256)} %constant.147.clone.1), kind=kCustom, calls=%fused_computation.41 | custom fusion | bytes 4915712 | tf_op jit(solution)/shard_map/scatter | solution.py:83
  106.7 496.8 %while.11 = (s32[]{:T(128)}, bf16[50,64,256]{2,1,0:T(8,128)(2,1)S(1)}, s32[50]{0:T(128)S(1)}, s32[50]{0:T(128)S(1)}, bf16[6,2,512,256]{2,3,1,0:T(8,128)(2,1)}, /...) while((s32[]{:T(128)}, ...), condition=%wide.region_16.17_spmd.clone, body=%wide.region_13.16_spmd.clone.sunk | while | flops 34737168 | bytes 3986795 | solution.py:117
  111.4 1.1 constant_dynamic-slice_fusion.4
  121.3 1.1 constant_dynamic-slice_fusion.4
  131.3 1.1 constant_dynamic-slice_fusion.4
  141.2 1.1 constant_dynamic-slice_fusion.4
  151.1 1.1 constant_dynamic-slice_fusion.4
  161.1 1.1 constant_dynamic-slice_fusion.4
  171.0 1.1 constant_dynamic-slice_fusion.4
  180.9 1.1 constant_dynamic-slice_fusion.4
  190.9 1.1 constant_dynamic-slice_fusion.4
  603.5 8.8 %gather_fusion.1 = bf16[2816,256]{1,0:T(8,128)(2,1)} fusion(bf16[3200,256]{1,0:T(8,128)(2,1)S(1)} %bitcast.113, s32[3072]{0:T(1024)S(1)} %pad_clamp_fusion), kind=kCustom, calls=%fused_computation.1 | custom fusion | bytes 2894848 | tf_op jit(solution)/shard_map/gather | solution.py:118
  612.3 2.5 fusion.15
  614.9 1.4 reshape.289
  616.3 4.7 all-to-all-start.2
  622.3 23.8 %all-to-all-done.2 = bf16[128,22,256]{2,1,0:T(8,128)(2,1)S(1)} async-done(((bf16[128,22,256]{2,1,0:T(8,128)(2,1)}), bf16[128,22,256]{2,1,0:T(8,128)(2,1)S(1)}, u32[]{:S(2)}, u32[]{:S(2)}) %all-to-all-start.2) | async-done | bytes 1441824 | tf_op jit(solution)/shard_map/all_to_all | solution.py:50
  646.5 2.9 fusion.21
  (1026 shorter events, 280.7 us)
Async XLA Ops:
  0.6 83.6 %copy-start = (bf16[256,768]{1,0:T(8,128)(2,1)S(1)}, bf16[256,768]{1,0:T(8,128)(2,1)}, u32[]{:S(2)}) copy-start(bf16[256,768]{1,0:T(8,128)(2,1)} %param.22) | copy-start | bytes 1179652
  0.6 7.4 %copy-start.3 = (s32[1024,1]{0,1:T(1,128)S(1)}, s32[1024,1]{0,1:T(1,128)}, u32[]{:S(2)}) copy-start(s32[1024,1]{0,1:T(1,128)} %param.14) | copy-start | bytes 12292
  0.7 0.8 copy-start.1
  0.7 7.4 %copy-start.7 = (s32[1024]{0:T(1024)S(1)}, s32[1024]{0:T(1024)}, u32[]{:S(2)}) copy-start(s32[1024]{0:T(1024)} %param.15) | copy-start | bytes 12292
  1.4 23.9 %copy-start.4 = (bf16[4,256]{1,0:T(4,128)(2,1)S(1)}, bf16[4,256]{1,0:T(4,128)(2,1)}, u32[]{:S(2)}) copy-start(bf16[4,256]{1,0:T(4,128)(2,1)} %param.18) | copy-start | bytes 6148
  9.0 26.8 %copy-start.5 = (s32[1024]{0:T(1024)}, s32[1024]{0:T(1024)S(1)}, u32[]{:S(2)}) copy-start(s32[1024]{0:T(1024)S(1)} %add_add_fusion) | copy-start | bytes 12292
  13.8 29.0 %all-to-all-start.1 = ((s32[128,1,22]{2,1,0:T(1,128)}), s32[128,1,22]{2,1,0:T(1,128)S(1)}, u32[]{:S(2)}, u32[]{:S(2)}) async-start(s32[128,1,22]{2,1,0:T(1,128)} %bitcast.8), calls=%async_computation.1 | async-start | bytes 131072 | tf_op jit(solution)/shard_map/all_to_all | solution.py:37
  25.4 8.4 %copy-start.13 = (s32[512]{0:T(512)S(1)}, s32[512]{0:T(512)}, u32[]{:S(2)}) copy-start(s32[512]{0:T(512)} %param.16) | copy-start | bytes 6148
  25.4 10.4 %copy-start.11 = (bf16[1024,48]{0,1:T(8,128)(2,1)S(1)}, bf16[1024,48]{0,1:T(8,128)(2,1)}, u32[]{:S(2)}) copy-start(bf16[1024,48]{0,1:T(8,128)(2,1)} %param.13) | copy-start | bytes 294916
  25.4 10.4 %copy-start.12 = (bf16[48,256]{1,0:T(8,128)(2,1)S(1)}, bf16[48,256]{1,0:T(8,128)(2,1)}, u32[]{:S(2)}) copy-start(bf16[48,256]{1,0:T(8,128)(2,1)} %param.20) | copy-start | bytes 73732
  25.4 16.3 %collective-permute-start = (bf16[2,256]{1,0:T(2,128)(2,1)S(1)}, bf16[2,256]{1,0:T(2,128)(2,1)S(1)}, u32[]{:S(2)}, u32[]{:S(2)}) collective-permute-start(bf16[2,256]{1,0:T(2,128)(2,1)S(1)} %slice.43), channel_id=1, source_target_pairs={{0,1},{1,2},{2,3},{3,4},{4,5},{5,6},{6,7},{7,8},{8,9},{9,10},{10,1... | collective-permute-start | bytes 3080 | tf_op jit(solution)/shard_map/ppermute | solution.py:12
  33.7 23.6 %collective-permute-start.1 = (bf16[2,2,512,256]{2,3,1,0:T(8,128)(2,1)}, bf16[2,2,512,256]{2,3,1,0:T(8,128)(2,1)}, u32[]{:S(2)}, u32[]{:S(2)}) collective-permute-start(bf16[2,2,512,256]{2,3,1,0:T(8,128)(2,1)} %slice.60), channel_id=1, source_target_pairs={{0,1},{1,2},{2,3},{3,4},{4,5},{5,6},{6,7},{7,8},{8,9},{9,10},{10,1... | collective-permute-start | bytes 3145736 | tf_op jit(solution)/shard_map/ppermute | solution.py:12
  41.8 11.4 %copy-start.8 = (bf16[2,256]{1,0:T(2,128)(2,1)}, bf16[2,256]{1,0:T(2,128)(2,1)S(1)}, u32[]{:S(2)}) copy-start(bf16[2,256]{1,0:T(2,128)(2,1)S(1)} %collective-permute-done) | copy-start | bytes 3076
  42.8 34.4 %all-to-all-start = ((bf16[128,22,256]{2,1,0:T(8,128)(2,1)}), bf16[128,22,256]{2,1,0:T(8,128)(2,1)}, u32[]{:S(2)}, u32[]{:S(2)}) async-start(bf16[128,22,256]{2,1,0:T(8,128)(2,1)} %reshape.285), calls=%async_computation | async-start | bytes 3145728 | tf_op jit(solution)/shard_map/all_to_all | solution.py:30
  84.3 3.4 copy-start.2
  87.6 19.0 %copy-start.14 = (s32[6]{0:T(128)S(1)}, s32[6]{0:T(128)}, u32[]{:S(2)}) copy-start(s32[6]{0:T(128)} %pad_add_fusion) | copy-start | bytes 76
  614.9 6.3 copy-start.9
  616.3 5.3 copy-start.10
  616.3 29.8 %all-to-all-start.2 = ((bf16[128,22,256]{2,1,0:T(8,128)(2,1)}), bf16[128,22,256]{2,1,0:T(8,128)(2,1)S(1)}, u32[]{:S(2)}, u32[]{:S(2)}) async-start(bf16[128,22,256]{2,1,0:T(8,128)(2,1)} %reshape.289), calls=%async_computation.2 | async-start | bytes 3145728 | tf_op jit(solution)/shard_map/all_to_all | solution.py:50
  621.0 25.5 %copy-start.6 = (s32[1024]{0:T(1024)S(1)}, s32[1024]{0:T(1024)}, u32[]{:S(2)}) copy-start(s32[1024]{0:T(1024)} %copy-done.5) | copy-start | bytes 12292
where the time goes:
time: 658 us; the launch traced here: 649 us
  loops' own time  217 us (33%)
  local copies, waits for them, and re-layouts  212 us (32%)
  other arithmetic  103 us (16%)
  matrix products  47.6 us (7%)
  waiting for transfers between devices  40 us (6%)
  starting transfers between devices  28 us (4%)
    another operation x1, loops' own time, score_rows(): lax.map(per_block, block_ids).reshape(block_total * block, width)  217 us
    slice x50, local copies, waits for them, and re-layouts, per_block(): keys = part[0].reshape(window, HEADS, head_dim)  53.5 us
    convert_element_type x50, other arithmetic, per_block(): group_v.astype(jnp.float32)  40.5 us
    dynamic_slice x50, local copies, waits for them, and re-layouts, score_rows(): lax.map(per_block, block_ids).reshape(block_total * block, width)  29.4 us
    dynamic_slice x50, local copies, waits for them, and re-layouts, per_block(): valid = positions < lengths[which]  27.8 us
    dynamic_slice x50, local copies, waits for them, and re-layouts, per_block(): which = block_slot[index]  27.7 us
    lt x50, other arithmetic, per_block(): valid = positions < lengths[which]  27.3 us
    all_to_all x1, waiting for transfers between devices, send_back(): lax.all_to_all(scored.reshape(n_ing * n_own, depth, width), ('ingest', 'o...  23.8 us
  transfers between devices with their start and end apart: 5, of which 2 were waited for; matrix products, arithmetic and copies ran while one was open for 4% of the time, Pallas kernels for 0%

commit v1 on v0

v1 whole, which is shorter than its diff:
```python
import functools

import jax
import jax.numpy as jnp
from jax import lax
from jax.experimental import pallas as pl
from jax.experimental.pallas import tpu as pltpu
from jax.sharding import PartitionSpec as P

HEADS = 4
MIG = 2
MESH = pl.DeviceIdType.MESH
F32 = jnp.float32
BF16 = jnp.bfloat16
I32 = jnp.int32


def iota(shape, dim):
    return lax.broadcasted_iota(I32, shape, dim)


def one_hot(mask):
    return jnp.where(mask, 1.0, 0.0).astype(BF16)


def mm(a, b):
    return jnp.dot(a, b, preferred_element_type=F32)


def kernel(
    n_ing,
    n_own,
    G,
    dev_ref,
    slot_ref,
    lens_ref,
    mig_ref,
    conv_ref,
    mel_ref,
    kv_ref,
    w_in_ref,
    w_state_ref,
    w_qkv_ref,
    w_out_ref,
    out_ref,
    new_ref,
    snd,
    rcv,
    rsnd,
    ret,
    kvb,
    kt,
    vc,
    mel2,
    um,
    ue,
    wx,
    sums,
    counts,
    upd_out,
    upd_in,
    kv_sem,
    ssem,
    rsem,
    bsem,
    csem,
    usem,
):
    devices = n_ing * n_own
    groups = devices // G
    rows = mel_ref.shape[1]
    mel = mel_ref.shape[0]
    sess, width = conv_ref.shape
    window = kv_ref.shape[2]
    ing = lax.axis_index("ingest")
    own = lax.axis_index("owner")
    me = ing * n_own + own
    grp = me // G

    def coords(p):
        return (p // n_own, p % n_own)

    kv_copy = pltpu.make_async_copy(kv_ref, kvb, kv_sem)
    kv_copy.start()

    barrier = pltpu.get_barrier_semaphore()

    def greet(i, c):
        p = lax.rem(me + i, devices)
        pl.semaphore_signal(barrier, inc=1, device_id=coords(p), device_id_type=MESH)
        return c

    lax.fori_loop(1, devices, greet, 0)

    dev = dev_ref[...]
    slot = slot_ref[...]
    step = 256
    upper = one_hot(iota((step, step), 0) < iota((step, step), 1))
    lane_dev = iota((devices, step), 0)
    carry = jnp.zeros((devices, 1), F32)
    ranks = []
    for b in range(rows // step):
        hit = jnp.where(lane_dev == dev[:, b * step : (b + 1) * step], 1.0, 0.0)
        before = mm(hit.astype(BF16), upper) + carry
        ranks.append(jnp.sum(before * hit, axis=0, keepdims=True))
        carry = carry + jnp.sum(hit, axis=1, keepdims=True)
    rank = jnp.concatenate(ranks, axis=1).astype(I32)
    code0 = jnp.where(rank < 8, dev * 8 + rank, -1)
    code1 = jnp.where(rank >= 8, dev * 8 + rank - 8, -1)
    code2 = jnp.where(rank >= 8, dev * 4 + rank - 8, -1)

    r16 = iota((16, rows), 0)
    slots = one_hot((r16 % 4 == slot) & (r16 < 12))
    half = jnp.concatenate([mel_ref[...], slots], axis=0)
    mel2[...] = jnp.concatenate([half, half], axis=0).T

    pl.semaphore_wait(barrier, devices - 1)

    tile = G * 8
    low = iota((tile, 128), 1) < 64

    def pack(j, c):
        g = lax.rem(grp + j, groups)
        at = iota((tile, rows), 0) + g * tile
        mels = mel2[...]
        first = mm(one_hot(at == code0), mels)
        second = mm(one_hot(at == code1), mels)
        packed = jnp.where(low, first, second).astype(BF16)
        snd[pl.ds(g * G, G)] = packed.reshape(G, 8, 128)

        def send(i, c):
            p = g * G + lax.rem(me + i, G)

            @pl.when(p != me)
            def _():
                pltpu.make_async_remote_copy(
                    src_ref=snd.at[p],
                    dst_ref=rcv.at[me],
                    send_sem=ssem,
                    recv_sem=rsem.at[grp],
                    device_id=coords(p),
                    device_id_type=MESH,
                ).start()

            return c

        lax.fori_loop(0, G, send, 0)
        return c

    lax.fori_loop(0, groups, pack, 0)
    rcv[pl.ds(me, 1)] = snd[pl.ds(me, 1)]

    r4 = iota((16, width), 0)
    states = mm(conv_ref[...], w_state_ref[...])
    tiled = jnp.zeros((16, width), F32)
    for s in range(sess):
        tiled = jnp.where(r4 % 4 == s, states[s : s + 1, :], tiled)
    hi = tiled.astype(BF16).astype(F32)
    mid = (tiled - hi).astype(BF16).astype(F32)
    lo = tiled - hi - mid
    terms = jnp.where(r4 < 4, hi, jnp.where(r4 < 8, mid, jnp.where(r4 < 12, lo, 0.0)))
    lanes4 = jnp.where((iota((16, width), 1) // 64 == r4) & (r4 < 4), 1.0, 0.0)
    r16l = iota((16, 128), 0)
    length = jnp.zeros((16, 128), I32)
    for s in range(sess):
        length = jnp.where(r16l % 4 == s, lens_ref[me * sess + s], length)
    length = jnp.where(
        r16l < 4, (length // 256) * 256, jnp.where(r16l < 8, length % 256, 0)
    ).astype(F32)
    wx[...] = jnp.zeros_like(wx)
    wx[0:mel, 0:width] = w_in_ref[...]
    wx[mel : mel + 16, :] = jnp.concatenate([terms, lanes4, length], axis=1).astype(BF16)

    kv_copy.wait()
    low_p = iota((window, 128), 1) < 64
    for pair in range(HEADS // 2):
        cols = slice(pair * 128, pair * 128 + 128)
        for sp in range(2):
            there = slice(sp * 128, sp * 128 + 128)
            for which in range(2):
                one = kvb[2 * sp, which, :, cols].astype(F32)
                two = kvb[2 * sp + 1, which, :, cols].astype(F32)
                even = jnp.where(low_p, one, pltpu.roll(two, 64, 1)).astype(BF16)
                odd = jnp.where(low_p, pltpu.roll(one, 64, 1), two).astype(BF16)
                if which == 0:
                    kt[2 * pair, there, :] = even.T
                    kt[2 * pair + 1, there, :] = odd.T
                else:
                    vc[2 * pair, :, there] = even
                    vc[2 * pair + 1, :, there] = odd

    diag = iota((128, 128), 0) == iota((128, 128), 1)
    for b in range(rows // 128):
        here = slice(b * 128, b * 128 + 128)
        c0 = jnp.sum(jnp.where(diag, code0[:, here].astype(F32), 0.0), axis=1, keepdims=True)
        c2 = jnp.sum(jnp.where(diag, code2[:, here].astype(F32), 0.0), axis=1, keepdims=True)
        um[here, :] = one_hot(iota((128, devices * 8), 1) == c0.astype(I32))
        ue[here, :] = one_hot(iota((128, devices * 4), 1) == c2.astype(I32))

    total = 12 * G
    sums[...] = jnp.zeros_like(sums)
    counts[...] = jnp.zeros_like(counts)
    pick = one_hot(
        (iota((4 * G, 8 * G), 0) // 4 == iota((4 * G, 8 * G), 1) // 8)
        & (iota((4 * G, 8 * G), 0) % 4 == iota((4 * G, 8 * G), 1) % 8)
    )
    slot_lane = one_hot((iota((8, 128), 1) == iota((8, 128), 0) + mel) & (iota((8, 128), 0) < sess))
    low_r = iota((total, 128), 1) < 64
    position = iota((total, window), 1)
    sub = iota((G // 2, 8, 128), 1) < 4

    def score(j, c):
        g = lax.rem(grp - j + groups, groups)

        @pl.when(j == 0)
        def _():
            part = rcv.at[pl.ds(g * G, G - 1)]
            pltpu.make_async_copy(part, part, rsem.at[g]).wait()

        @pl.when(j > 0)
        def _():
            part = rcv.at[pl.ds(g * G, G)]
            pltpu.make_async_copy(part, part, rsem.at[g]).wait()

        a = rcv[pl.ds(g * G, G)].reshape(8 * G, 128)
        x = pltpu.roll(mm(pick, a), 64, 1).astype(BF16)
        both = jnp.concatenate([a, x], axis=0)
        f = mm(both, wx[...])
        pre = f[:, :width]
        mask4 = f[:, width : 2 * width]
        valid = position < f[:, 2 * width : 2 * width + 1].astype(I32)
        hidden = (pre * jax.nn.sigmoid(pre)).astype(BF16)
        qkv = mm(hidden, w_qkv_ref[...])
        outs = []
        for pair in range(HEADS // 2):
            cols = slice(pair * 128, pair * 128 + 128)
            q = qkv[:, pair * 128 : pair * 128 + 128].astype(BF16).astype(F32) * 0.125
            k = qkv[:, width + pair * 128 : width + pair * 128 + 128].astype(BF16).astype(F32)
            v = qkv[:, 2 * width + pair * 128 : 2 * width + pair * 128 + 128]
            v = v.astype(BF16).astype(F32)
            turned = pltpu.roll(q, 64, 1)
            halves = (jnp.where(low_r, q, turned), jnp.where(low_r, turned, q))
            mixed, tops, totals = [], [], []
            for h in range(2):
                wide = (jnp.concatenate([halves[h], halves[h]], axis=1) * mask4).astype(BF16)
                s = jnp.where(valid, mm(wide, kt[2 * pair + h]), -1e30)
                top = jnp.max(s, axis=1, keepdims=True)
                e = jnp.exp(s - top)
                totals.append(jnp.sum(e, axis=1, keepdims=True))
                tops.append(top)
                o = mm(e.astype(BF16), vc[2 * pair + h]) * mask4
                mixed.append(o[:, :128] + o[:, 128:])
            mix = jnp.where(low_r, mixed[0], mixed[1]) + pltpu.roll(
                jnp.where(low_r, mixed[1], mixed[0]), 64, 1
            )
            top = jnp.where(low_r, tops[0], tops[1])
            tot = jnp.where(low_r, totals[0], totals[1])
            prod = q * k
            own0 = jnp.sum(jnp.where(low_r, prod, 0.0), axis=1, keepdims=True)
            own1 = jnp.sum(jnp.where(low_r, 0.0, prod), axis=1, keepdims=True)
            mine = jnp.where(low_r, own0, own1)
            peak = jnp.maximum(top, mine)
            ea = jnp.exp(top - peak)
            eb = jnp.exp(mine - peak)
            outs.append(((ea * mix + eb * v) / (ea * tot + eb)).astype(BF16))
        attn = jnp.concatenate(outs, axis=1)
        scored = (hidden.astype(F32) + mm(attn, w_out_ref[...])).astype(BF16)
        wide = scored.astype(F32)
        first = pl.ds(g * G, G)
        rsnd[first, 0:8, :] = scored[: 8 * G, :128].reshape(G, 8, 128)
        rsnd[first, 8:16, :] = scored[: 8 * G, 128:].reshape(G, 8, 128)
        left = wide[8 * G :, :128].reshape(G // 2, 8, 128)
        right = wide[8 * G :, 128:].reshape(G // 2, 8, 128)
        ones = jnp.where(sub, left, pltpu.roll(right, 4, 1))
        twos = jnp.where(sub, pltpu.roll(left, 4, 1), right)
        rsnd[first, 16:24, :] = jnp.stack([ones, twos], axis=1).reshape(G, 8, 128).astype(BF16)

        def back(i, c):
            p = g * G + lax.rem(me + i, G)

            @pl.when(p != me)
            def _():
                pltpu.make_async_remote_copy(
                    src_ref=rsnd.at[p],
                    dst_ref=ret.at[me],
                    send_sem=bsem,
                    recv_sem=csem,
                    device_id=coords(p),
                    device_id_type=MESH,
                ).start()

            return c

        lax.fori_loop(0, G, back, 0)
        marks = lax.dot_general(
            slot_lane, both, (((1,), (1,)), ((), ())), preferred_element_type=F32
        )
        sums[...] += mm(marks.astype(BF16), scored)
        counts[...] += jnp.sum(marks, axis=1, keepdims=True)
        return c

    lax.fori_loop(0, groups, score, 0)
    ret[pl.ds(me, 1)] = rsnd[pl.ds(me, 1)]

    n = counts[0:sess, 0:1]
    mean = sums[0:sess, :] / jnp.maximum(n, 1.0)
    updated = jnp.where(n > 0, mean, conv_ref[...].astype(F32)).astype(BF16).astype(F32)
    upd_out[...] = jnp.zeros_like(upd_out)
    upd_out[0:sess, :] = updated
    push = pltpu.make_async_remote_copy(
        src_ref=upd_out,
        dst_ref=upd_in,
        send_sem=usem.at[0],
        recv_sem=usem.at[1],
        device_id=(ing, lax.rem(own + 1, n_own)),
        device_id_type=MESH,
    )
    push.start()
    push.wait()
    r8 = iota((8, width), 0)
    prev = ing * n_own + lax.rem(own + n_own - 1, n_own)
    keep = (r8 < sess) & (r8 < sess - mig_ref[me])
    live = (r8 >= sess) & (r8 - sess >= MIG - mig_ref[prev])
    table = jnp.where(
        keep, upd_out[...], jnp.where(live, pltpu.roll(upd_in[...], MIG, 0), 0.0)
    ).astype(BF16)
    new_ref[...] = table[0 : sess + MIG, :]

    other = snd.at[pl.ds(0, devices - 1)]
    pltpu.make_async_copy(other, other, ssem).wait()
    other = rsnd.at[pl.ds(0, devices - 1)]
    pltpu.make_async_copy(other, other, bsem).wait()
    other = ret.at[pl.ds(0, devices - 1)]
    pltpu.make_async_copy(other, other, csem).wait()
    main = jnp.concatenate(
        [
            ret[:, 0:8, :].reshape(devices * 8, 128),
            ret[:, 8:16, :].reshape(devices * 8, 128),
        ],
        axis=1,
    )
    extra = ret[:, 16:24, :].astype(F32).reshape(devices // 2, 2, 8, 128)
    ones, twos = extra[:, 0], extra[:, 1]
    sub = iota((devices // 2, 8, 128), 1) < 4
    left = jnp.where(sub, ones, pltpu.roll(twos, 4, 1)).reshape(devices * 4, 128)
    right = jnp.where(sub, pltpu.roll(ones, 4, 1), twos).reshape(devices * 4, 128)
    extra = jnp.concatenate([left, right], axis=1).astype(BF16)
    for b in range(rows // 256):
        here = slice(b * 256, b * 256 + 256)
        out_ref[here, :] = (mm(um[here, :], main) + mm(ue[here, :], extra)).astype(BF16)


def body(
    frame_mel,
    row_device,
    row_slot,
    window_length,
    migrate_count,
    conv_state,
    kv_cache,
    w_in,
    w_state,
    w_qkv,
    w_out,
):
    n_ing = lax.axis_size("ingest")
    n_own = lax.axis_size("owner")
    devices = n_ing * n_own
    rows, mel = frame_mel.shape
    sess, _, window, width = kv_cache.shape
    G = 16
    groups = devices // G
    vmem = pl.BlockSpec(memory_space=pltpu.VMEM)
    smem = pl.BlockSpec(memory_space=pltpu.SMEM)
    return pl.pallas_call(
        functools.partial(kernel, n_ing, n_own, G),
        out_shape=(
            jax.ShapeDtypeStruct((rows, width), BF16),
            jax.ShapeDtypeStruct((sess + MIG, width), BF16),
        ),
        in_specs=[
            vmem,
            vmem,
            smem,
            smem,
            vmem,
            vmem,
            pl.BlockSpec(memory_space=pl.ANY),
            vmem,
            vmem,
            vmem,
            vmem,
        ],
        out_specs=(vmem, vmem),
        scratch_shapes=[
            pltpu.VMEM((devices, 8, 128), BF16),
            pltpu.VMEM((devices, 8, 128), BF16),
            pltpu.VMEM((devices, 24, 128), BF16),
            pltpu.VMEM((devices, 24, 128), BF16),
            pltpu.VMEM(kv_cache.shape, BF16),
            pltpu.VMEM((HEADS, width, window), BF16),
            pltpu.VMEM((HEADS, window, width), BF16),
            pltpu.VMEM((rows, 128), BF16),
            pltpu.VMEM((rows, devices * 8), BF16),
            pltpu.VMEM((rows, devices * 4), BF16),
            pltpu.VMEM((128, 2 * width + 128), BF16),
            pltpu.VMEM((8, width), F32),
            pltpu.VMEM((8, 128), F32),
            pltpu.VMEM((8, width), F32),
            pltpu.VMEM((8, width), F32),
            pltpu.SemaphoreType.DMA,
            pltpu.SemaphoreType.DMA,
            pltpu.SemaphoreType.DMA((groups,)),
            pltpu.SemaphoreType.DMA,
            pltpu.SemaphoreType.DMA,
            pltpu.SemaphoreType.DMA((2,)),
        ],
        compiler_params=pltpu.CompilerParams(
            collective_id=0, has_side_effects=True, vmem_limit_bytes=56 << 20
        ),
        name="scorer",
    )(
        row_device.reshape(1, rows),
        row_slot.reshape(1, rows),
        window_length,
        migrate_count,
        conv_state,
        frame_mel.T,
        kv_cache,
        w_in,
        w_state,
        w_qkv,
        w_out,
    )


def solution(mesh):
    placed = (
        P(("ingest", "owner"), None),
        P(("ingest", "owner"), None),
        P(("ingest", "owner")),
        P(),
        P(),
        P(("ingest", "owner"), None),
        P(("ingest", "owner"), None, None, None),
        P(),
        P(),
        P(),
        P(),
    )
    return jax.shard_map(
        body,
        mesh=mesh,
        in_specs=placed,
        out_specs=(P(("ingest", "owner"), None), P(("ingest", "owner"), None)),
        check_vma=False,
    )
```

time: 658 us -> 49.2 us (0.07); the launches traced: 649 us -> 49 us
  loops' own time: 217 us -> 0 us
  local copies, waits for them, and re-layouts: 212 us -> 3.13 us
  other arithmetic: 103 us -> 0 us
  matrix products: 47.6 us -> 0 us
  Pallas kernels: 0 us -> 45.2 us
  waiting for transfers between devices: 40 us -> 0 us
  starting transfers between devices: 28 us -> 0 us
    another operation x1 -> x0, loops' own time: 217 us -> none  [score_rows(): lax.map(per_block, block_ids).reshape(block_total * block, width)]
    dynamic_slice x153 -> x0, local copies, waits for them, and re-layouts: 85.6 us -> none  [the longest x50 29.4 us: score_rows(): lax.map(per_block, block_ids).reshape(block_total * block, width)]
    slice x52 -> x0, local copies, waits for them, and re-layouts: 55.8 us -> none  [the longest x50 53.5 us: per_block(): keys = part[0].reshape(window, HEADS, head_dim)]
    dot_general x107 -> x0, matrix products: 47.6 us -> none  [the longest x50 16.4 us: per_block(): jnp.einsum('hrp,phd->rhd', weights, values, preferred_element_type=jnp.fl...]
    pallas_call x0 -> x1, Pallas kernels: none -> 45.2 us  [body(): pl.pallas_call(functools.partial(kernel, n_ing, n_own, G), out_shape=(jax...]
    convert_element_type x101 -> x0, other arithmetic: 41.1 us -> none  [the longest x50 40.5 us: per_block(): group_v.astype(jnp.float32)]
    all_to_all x3 -> x0, waiting for transfers between devices: 40 us -> none  [the longest x1 23.8 us: send_back(): lax.all_to_all(scored.reshape(n_ing * n_own, depth, width), ('ingest', 'o...]
    lt x51 -> x0, other arithmetic: 27.9 us -> none  [the longest x50 27.3 us: per_block(): valid = positions < lengths[which]]
  transfers between devices with their start and end apart: 5 -> 0, of which waited for: 2 -> 0; matrix products, arithmetic and copies ran while one was open for 4% -> 0% of each run, Pallas kernels for 0% -> 0%
where the time goes in v1:
time: 49.2 us; the launch traced here: 49 us
  Pallas kernels  45.2 us (92%)
  local copies, waits for them, and re-layouts  3.13 us (6%)
  between operations  0.64 us (1%)
    pallas_call x1, Pallas kernels, body(): pl.pallas_call(functools.partial(kernel, n_ing, n_own, G), out_shape=(jax...  45.2 us
    unnamed x2, local copies, waits for them, and re-layouts  3.13 us

profile of v1, /device:TPU:1, one launch (start us, length us, event | category | flops | bytes accessed | tf_op | source)
XLA Modules:
  0.0 49.0 jit_solution(1902557895106408324)
XLA Ops:
  0.6 45.2 %scorer.1 = (bf16[1024,256]{1,0:T(8,128)(2,1)}, bf16[6,256]{1,0:T(8,128)(2,1)}) custom-call(s32[1,1024]{1,0:T(1,128)} %bitcast.4, s32[1,1024]{1,0:T(1,128)} %bitcast.5, s32[512]{0:T(512)} %lens_ref.1, s32[128]{0:T(128)} %mig_ref.1, bf16[4,256]{1,0:T(4,128)(2,1)} %conv_ref.1, bf16[48,1024]{1,0:T(8,128)(2,1)} %bitcast.3, bf16[4,2,512,256]{3,2,1,0:T(8,128)(2,1)} %kv_ref.1, ...), custom_call_target="tpu_custom_call" | custom-call | tf_op jit(solution)/shard_map/scorer/pallas_call | solution.py:375
  45.9 1.9 %copy.15 = bf16[1024,256]{1,0:T(8,128)(2,1)} copy(bf16[1024,256]{1,0:T(8,128)(2,1)} %get-tuple-element.4) | data formatting | bytes 1048576
  47.7 1.3 %copy.16 = bf16[6,256]{1,0:T(8,128)(2,1)} copy(bf16[6,256]{1,0:T(8,128)(2,1)} %get-tuple-element.5) | data formatting | bytes 6144

commit v2 on v1

--- a/solution.py
+++ b/solution.py
@@ -55,10 +55,12 @@
     um,
     ue,
     wx,
+    wq,
     sums,
     counts,
     upd_out,
     upd_in,
+    acc,
     kv_sem,
     ssem,
     rsem,
@@ -75,10 +77,32 @@
     ing = lax.axis_index("ingest")
     own = lax.axis_index("owner")
     me = ing * n_own + own
-    grp = me // G
-
-    def coords(p):
-        return (p // n_own, p % n_own)
+
+    N = n_ing
+    yy, zz, core = own // (2 * N), (own // 2) % N, own % 2
+    mine_k = (ing + yy + zz) % N
+    place = mine_k * G + ing * (2 * N) + yy * 2 + core
+
+    def peer(k, dx, dy, dc):
+        x, y, c = (ing + dx) % N, (yy + dy) % N, (core + dc) % 2
+        z = (k + 2 * N - x - y) % N
+        return k * G + x * (2 * N) + y * 2 + c, (x, y * (2 * N) + z * 2 + c)
+
+    def each_peer(j, k, start):
+        def step(dx, c):
+            for dy in range(N):
+                for dc in range(2):
+                    if dy + dc > 0:
+                        start(*peer(k, dx, dy, dc))
+            return c
+
+        lax.fori_loop(0, N, step, 0)
+        for dx in range(1, N):
+            start(*peer(k, dx, 0, 0))
+
+        @pl.when(j > 0)
+        def _():
+            start(*peer(k, 0, 0, 0))
 
     kv_copy = pltpu.make_async_copy(kv_ref, kvb, kv_sem)
     kv_copy.start()
@@ -86,11 +110,16 @@
     barrier = pltpu.get_barrier_semaphore()
 
     def greet(i, c):
-        p = lax.rem(me + i, devices)
-        pl.semaphore_signal(barrier, inc=1, device_id=coords(p), device_id_type=MESH)
+        for a in range(n_ing):
+            x = lax.rem(ing + a, n_ing)
+            y = lax.rem(own + i, n_own)
+            pl.semaphore_signal(barrier, inc=1, device_id=(x, y), device_id_type=MESH)
         return c
 
-    lax.fori_loop(1, devices, greet, 0)
+    lax.fori_loop(1, n_own, greet, 0, unroll=4)
+    for a in range(1, n_ing):
+        x = lax.rem(ing + a, n_ing)
+        pl.semaphore_signal(barrier, inc=1, device_id=(x, own), device_id_type=MESH)
 
     dev = dev_ref[...]
     slot = slot_ref[...]
@@ -105,9 +134,11 @@
         ranks.append(jnp.sum(before * hit, axis=0, keepdims=True))
         carry = carry + jnp.sum(hit, axis=1, keepdims=True)
     rank = jnp.concatenate(ranks, axis=1).astype(I32)
-    code0 = jnp.where(rank < 8, dev * 8 + rank, -1)
-    code1 = jnp.where(rank >= 8, dev * 8 + rank - 8, -1)
-    code2 = jnp.where(rank >= 8, dev * 4 + rank - 8, -1)
+    x, y, z = dev // n_own, (dev // (2 * N)) % N, (dev // 2) % N
+    spot = (x + y + z) % N * G + x * (2 * N) + y * 2 + dev % 2
+    code0 = jnp.where(rank < 8, spot * 8 + rank, -1)
+    code1 = jnp.where(rank >= 8, spot * 8 + rank - 8, -1)
+    code2 = jnp.where(rank >= 8, spot * 4 + rank - 8, -1)
 
     r16 = iota((16, rows), 0)
     slots = one_hot((r16 % 4 == slot) & (r16 < 12))
@@ -118,37 +149,42 @@
 
     tile = G * 8
     low = iota((tile, 128), 1) < 64
+    lines = jnp.concatenate([iota((tile, 128), 0).astype(F32).astype(BF16)] * (rows // 128), axis=1)
+
+    def spread(code, g):
+        code = jnp.broadcast_to((code - g * tile).astype(F32), (16, rows)).astype(BF16)
+        return jnp.concatenate([code] * (tile // 16), axis=0)
+
+    one, zero = jnp.ones((), BF16), jnp.zeros((), BF16)
+
+    def send(slot_, to):
+        pltpu.make_async_remote_copy(
+            src_ref=snd.at[slot_],
+            dst_ref=rcv.at[place],
+            send_sem=ssem,
+            recv_sem=rsem.at[mine_k],
+            device_id=to,
+            device_id_type=MESH,
+        ).start()
 
     def pack(j, c):
-        g = lax.rem(grp + j, groups)
-        at = iota((tile, rows), 0) + g * tile
-        mels = mel2[...]
-        first = mm(one_hot(at == code0), mels)
-        second = mm(one_hot(at == code1), mels)
-        packed = jnp.where(low, first, second).astype(BF16)
+        g = (mine_k + j) % groups
+        picks = jnp.concatenate(
+            [
+                jnp.where(lines == spread(code0, g), one, zero),
+                jnp.where(lines == spread(code1, g), one, zero),
+            ],
+            axis=0,
+        )
+        both = mm(picks, mel2[...])
+        packed = jnp.where(low, both[:tile], both[tile:]).astype(BF16)
         snd[pl.ds(g * G, G)] = packed.reshape(G, 8, 128)
 
-        def send(i, c):
-            p = g * G + lax.rem(me + i, G)
-
-            @pl.when(p != me)
-            def _():
-                pltpu.make_async_remote_copy(
-                    src_ref=snd.at[p],
-                    dst_ref=rcv.at[me],
-                    send_sem=ssem,
-                    recv_sem=rsem.at[grp],
-                    device_id=coords(p),
-                    device_id_type=MESH,
-                ).start()
-
-            return c
-
-        lax.fori_loop(0, G, send, 0)
+        each_peer(j, g, send)
         return c
 
     lax.fori_loop(0, groups, pack, 0)
-    rcv[pl.ds(me, 1)] = snd[pl.ds(me, 1)]
+    rcv[pl.ds(place, 1)] = snd[pl.ds(place, 1)]
 
     r4 = iota((16, width), 0)
     states = mm(conv_ref[...], w_state_ref[...])
@@ -160,28 +196,49 @@
     lo = tiled - hi - mid
     terms = jnp.where(r4 < 4, hi, jnp.where(r4 < 8, mid, jnp.where(r4 < 12, lo, 0.0)))
     lanes4 = jnp.where((iota((16, width), 1) // 64 == r4) & (r4 < 4), 1.0, 0.0)
-    r16l = iota((16, 128), 0)
-    length = jnp.zeros((16, 128), I32)
-    for s in range(sess):
-        length = jnp.where(r16l % 4 == s, lens_ref[me * sess + s], length)
-    length = jnp.where(
-        r16l < 4, (length // 256) * 256, jnp.where(r16l < 8, length % 256, 0)
-    ).astype(F32)
+    lengths = [lens_ref[me * sess + s] for s in range(sess)]
     wx[...] = jnp.zeros_like(wx)
     wx[0:mel, 0:width] = w_in_ref[...]
-    wx[mel : mel + 16, :] = jnp.concatenate([terms, lanes4, length], axis=1).astype(BF16)
+    wx[mel : mel + 16, :] = jnp.concatenate([terms, lanes4], axis=1).astype(BF16)
+    lane = iota((1, width), 1)
+    past = jnp.zeros((1, width), F32)
+    for s in range(sess):
+        past = jnp.where(lane == 64 * s, (window - lengths[s]).astype(F32), past)
+
+    low_w = iota((width, 128), 1) < 64
+    for pair in range(HEADS // 2):
+        w = w_qkv_ref[:, pair * 128 : pair * 128 + 128].astype(F32) * 0.125
+        turned = pltpu.roll(w, 64, 1)
+        wq[:, pair * 256 : pair * 256 + 128] = jnp.where(low_w, w, turned).astype(BF16)
+        wq[:, pair * 256 + 128 : pair * 256 + 256] = jnp.where(low_w, turned, w).astype(BF16)
+    wq[:, 2 * width :] = w_qkv_ref[:, width:]
 
     kv_copy.wait()
     low_p = iota((window, 128), 1) < 64
-    for pair in range(HEADS // 2):
-        cols = slice(pair * 128, pair * 128 + 128)
-        for sp in range(2):
-            there = slice(sp * 128, sp * 128 + 128)
+    row_p = iota((window, 128), 0)
+
+    def turn(a, by):
+        return jnp.concatenate([a[window - by :], a[: window - by]], axis=0) if by else a
+
+    for sp in range(2):
+        there = slice(sp * 128, sp * 128 + 128)
+        in_one = row_p < lengths[2 * sp]
+        in_two = row_p < lengths[2 * sp + 1]
+        for pair in range(HEADS // 2):
+            cols = slice(pair * 128, pair * 128 + 128)
             for which in range(2):
-                one = kvb[2 * sp, which, :, cols].astype(F32)
-                two = kvb[2 * sp + 1, which, :, cols].astype(F32)
-                even = jnp.where(low_p, one, pltpu.roll(two, 64, 1)).astype(BF16)
-                odd = jnp.where(low_p, pltpu.roll(one, 64, 1), two).astype(BF16)
+                one_ = kvb[2 * sp, which, :, cols].astype(F32)
+                two_ = kvb[2 * sp + 1, which, :, cols].astype(F32)
+                if which == 0:
+                    one_ = jnp.where(in_one, one_, one_[0:1, :])
+                    two_ = jnp.where(in_two, two_, two_[0:1, :])
+                else:
+                    one_ = jnp.where(in_one, one_, 0.0)
+                    two_ = jnp.where(in_two, two_, 0.0)
+                one_ = turn(one_, 64 * (2 * sp))
+                two_ = turn(two_, 64 * (2 * sp + 1))
+                even = jnp.where(low_p, one_, pltpu.roll(two_, 64, 1)).astype(BF16)
+                odd = jnp.where(low_p, pltpu.roll(one_, 64, 1), two_).astype(BF16)
                 if which == 0:
                     kt[2 * pair, there, :] = even.T
                     kt[2 * pair + 1, there, :] = odd.T
@@ -194,8 +251,13 @@
         here = slice(b * 128, b * 128 + 128)
         c0 = jnp.sum(jnp.where(diag, code0[:, here].astype(F32), 0.0), axis=1, keepdims=True)
         c2 = jnp.sum(jnp.where(diag, code2[:, here].astype(F32), 0.0), axis=1, keepdims=True)
-        um[here, :] = one_hot(iota((128, devices * 8), 1) == c0.astype(I32))
-        ue[here, :] = one_hot(iota((128, devices * 4), 1) == c2.astype(I32))
+        across = iota((128, 256), 1).astype(F32).astype(BF16)
+        for t in range(devices * 8 // 256):
+            near = jnp.broadcast_to(c0 - t * 256, (128, 256)).astype(BF16)
+            um[here, t * 256 : t * 256 + 256] = jnp.where(across == near, one, zero)
+        for t in range(devices * 4 // 256):
+            near = jnp.broadcast_to(c2 - t * 256, (128, 256)).astype(BF16)
+            ue[here, t * 256 : t * 256 + 256] = jnp.where(across == near, one, zero)
 
     total = 12 * G
     sums[...] = jnp.zeros_like(sums)
@@ -206,11 +268,10 @@
     )
     slot_lane = one_hot((iota((8, 128), 1) == iota((8, 128), 0) + mel) & (iota((8, 128), 0) < sess))
     low_r = iota((total, 128), 1) < 64
-    position = iota((total, window), 1)
     sub = iota((G // 2, 8, 128), 1) < 4
 
     def score(j, c):
-        g = lax.rem(grp - j + groups, groups)
+        g = (mine_k + groups - j) % groups
 
         @pl.when(j == 0)
         def _():
@@ -227,35 +288,37 @@
         both = jnp.concatenate([a, x], axis=0)
         f = mm(both, wx[...])
         pre = f[:, :width]
-        mask4 = f[:, width : 2 * width]
-        valid = position < f[:, 2 * width : 2 * width + 1].astype(I32)
+        in_lanes = f[:, width : 2 * width]
+        mask4 = in_lanes.astype(BF16)
+        spare = in_lanes * past
         hidden = (pre * jax.nn.sigmoid(pre)).astype(BF16)
-        qkv = mm(hidden, w_qkv_ref[...])
+        qkv = mm(hidden, wq[...])
         outs = []
         for pair in range(HEADS // 2):
-            cols = slice(pair * 128, pair * 128 + 128)
-            q = qkv[:, pair * 128 : pair * 128 + 128].astype(BF16).astype(F32) * 0.125
-            k = qkv[:, width + pair * 128 : width + pair * 128 + 128].astype(BF16).astype(F32)
-            v = qkv[:, 2 * width + pair * 128 : 2 * width + pair * 128 + 128]
-            v = v.astype(BF16).astype(F32)
-            turned = pltpu.roll(q, 64, 1)
-            halves = (jnp.where(low_r, q, turned), jnp.where(low_r, turned, q))
-            mixed, tops, totals = [], [], []
+            kcol = 2 * width + pair * 128
+            k = qkv[:, kcol : kcol + 128]
+            v = qkv[:, kcol + width : kcol + width + 128]
+            mixed, tops, totals, qs = [], [], [], []
             for h in range(2):
-                wide = (jnp.concatenate([halves[h], halves[h]], axis=1) * mask4).astype(BF16)
-                s = jnp.where(valid, mm(wide, kt[2 * pair + h]), -1e30)
+                at = pair * 256 + h * 128
+                qs.append(qkv[:, at : at + 128])
+                q = qs[h].astype(BF16)
+                wide = jnp.concatenate([q, q], axis=1) * mask4
+                s = mm(wide, kt[2 * pair + h])
                 top = jnp.max(s, axis=1, keepdims=True)
                 e = jnp.exp(s - top)
-                totals.append(jnp.sum(e, axis=1, keepdims=True))
+                part = (e[:, :128] + e[:, 128:256]) + (e[:, 256:384] + e[:, 384:])
+                part = part - spare[:, :128] * e[:, :128] - spare[:, 128:] * e[:, 128:256]
+                totals.append(jnp.sum(part, axis=1, keepdims=True))
                 tops.append(top)
-                o = mm(e.astype(BF16), vc[2 * pair + h]) * mask4
-                mixed.append(o[:, :128] + o[:, 128:])
+                o = mm(e.astype(BF16), vc[2 * pair + h])
+                mixed.append(o[:, :128] * in_lanes[:, :128] + o[:, 128:] * in_lanes[:, 128:])
             mix = jnp.where(low_r, mixed[0], mixed[1]) + pltpu.roll(
                 jnp.where(low_r, mixed[1], mixed[0]), 64, 1
             )
             top = jnp.where(low_r, tops[0], tops[1])
             tot = jnp.where(low_r, totals[0], totals[1])
-            prod = q * k
+            prod = jnp.where(low_r, qs[0], qs[1]) * k
             own0 = jnp.sum(jnp.where(low_r, prod, 0.0), axis=1, keepdims=True)
             own1 = jnp.sum(jnp.where(low_r, 0.0, prod), axis=1, keepdims=True)
             mine = jnp.where(low_r, own0, own1)
@@ -275,23 +338,17 @@
         twos = jnp.where(sub, pltpu.roll(left, 4, 1), right)
         rsnd[first, 16:24, :] = jnp.stack([ones, twos], axis=1).reshape(G, 8, 128).astype(BF16)
 
-        def back(i, c):
-            p = g * G + lax.rem(me + i, G)
-
-            @pl.when(p != me)
-            def _():
-                pltpu.make_async_remote_copy(
-                    src_ref=rsnd.at[p],
-                    dst_ref=ret.at[me],
-                    send_sem=bsem,
-                    recv_sem=csem,
-                    device_id=coords(p),
-                    device_id_type=MESH,
-                ).start()
-
-            return c
-
-        lax.fori_loop(0, G, back, 0)
+        def back(slot_, to):
+            pltpu.make_async_remote_copy(
+                src_ref=rsnd.at[slot_],
+                dst_ref=ret.at[place],
+                send_sem=bsem,
+                recv_sem=csem.at[mine_k],
+                device_id=to,
+                device_id_type=MESH,
+            ).start()
+
+        each_peer(j, g, back)
         marks = lax.dot_general(
             slot_lane, both, (((1,), (1,)), ((), ())), preferred_element_type=F32
         )
@@ -300,7 +357,7 @@
         return c
 
     lax.fori_loop(0, groups, score, 0)
-    ret[pl.ds(me, 1)] = rsnd[pl.ds(me, 1)]
+    ret[pl.ds(place, 1)] = rsnd[pl.ds(place, 1)]
 
     n = counts[0:sess, 0:1]
     mean = sums[0:sess, :] / jnp.maximum(n, 1.0)
@@ -316,6 +373,57 @@
         device_id_type=MESH,
     )
     push.start()
+    sub = iota((G // 2, 8, 128), 1) < 4
+
+    def unpack(j, c):
+        k = (mine_k + j) % groups
+
+        @pl.when(j == 0)
+        def _():
+            part = ret.at[pl.ds(k * G, G - 1)]
+            pltpu.make_async_copy(part, part, csem.at[k]).wait()
+
+        @pl.when(j > 0)
+        def _():
+            part = ret.at[pl.ds(k * G, G)]
+            pltpu.make_async_copy(part, part, csem.at[k]).wait()
+
+        here = pl.ds(k * G, G)
+        main = jnp.concatenate(
+            [
+                ret[here, 0:8, :].reshape(G * 8, 128),
+                ret[here, 8:16, :].reshape(G * 8, 128),
+            ],
+            axis=1,
+        )
+        extra = ret[here, 16:24, :].astype(F32).reshape(G // 2, 2, 8, 128)
+        ones, twos = extra[:, 0], extra[:, 1]
+        left = jnp.where(sub, ones, pltpu.roll(twos, 4, 1)).reshape(G * 4, 128)
+        right = jnp.where(sub, pltpu.roll(ones, 4, 1), twos).reshape(G * 4, 128)
+        extra = jnp.concatenate([left, right], axis=1).astype(BF16)
+        mains = um[:, pl.ds(pl.multiple_of(k * (G * 8), 256), G * 8)]
+        extras = ue[:, pl.ds(pl.multiple_of(k * (G * 4), 128), G * 4)]
+        more = mm(mains, main) + mm(extras, extra)
+
+        @pl.when(j == 0)
+        def _():
+            acc[...] = more
+
+        @pl.when((j > 0) & (j < groups - 1))
+        def _():
+            acc[...] += more
+
+        @pl.when(j == groups - 1)
+        def _():
+            out_ref[...] = (acc[...] + more).astype(BF16)
+
+        return c
+
+    lax.fori_loop(0, groups, unpack, 0)
+    other = snd.at[pl.ds(0, devices - 1)]
+    pltpu.make_async_copy(other, other, ssem).wait()
+    other = rsnd.at[pl.ds(0, devices - 1)]
+    pltpu.make_async_copy(other, other, bsem).wait()
     push.wait()
     r8 = iota((8, width), 0)
     prev = ing * n_own + lax.rem(own + n_own - 1, n_own)
@@ -325,29 +433,6 @@
         keep, upd_out[...], jnp.where(live, pltpu.roll(upd_in[...], MIG, 0), 0.0)
     ).astype(BF16)
     new_ref[...] = table[0 : sess + MIG, :]
-
-    other = snd.at[pl.ds(0, devices - 1)]
-    pltpu.make_async_copy(other, other, ssem).wait()
-    other = rsnd.at[pl.ds(0, devices - 1)]
-    pltpu.make_async_copy(other, other, bsem).wait()
-    other = ret.at[pl.ds(0, devices - 1)]
-    pltpu.make_async_copy(other, other, csem).wait()
-    main = jnp.concatenate(
-        [
-            ret[:, 0:8, :].reshape(devices * 8, 128),
-            ret[:, 8:16, :].reshape(devices * 8, 128),
-        ],
-        axis=1,
-    )
-    extra = ret[:, 16:24, :].astype(F32).reshape(devices // 2, 2, 8, 128)
-    ones, twos = extra[:, 0], extra[:, 1]
-    sub = iota((devices // 2, 8, 128), 1) < 4
-    left = jnp.where(sub, ones, pltpu.roll(twos, 4, 1)).reshape(devices * 4, 128)
-    right = jnp.where(sub, pltpu.roll(ones, 4, 1), twos).reshape(devices * 4, 128)
-    extra = jnp.concatenate([left, right], axis=1).astype(BF16)
-    for b in range(rows // 256):
-        here = slice(b * 256, b * 256 + 256)
-        out_ref[here, :] = (mm(um[here, :], main) + mm(ue[here, :], extra)).astype(BF16)
 
 
 def body(
@@ -368,7 +453,7 @@
     devices = n_ing * n_own
     rows, mel = frame_mel.shape
     sess, _, window, width = kv_cache.shape
-    G = 16
+    G = n_own
     groups = devices // G
     vmem = pl.BlockSpec(memory_space=pltpu.VMEM)
     smem = pl.BlockSpec(memory_space=pltpu.SMEM)
@@ -403,16 +488,18 @@
             pltpu.VMEM((rows, 128), BF16),
             pltpu.VMEM((rows, devices * 8), BF16),
             pltpu.VMEM((rows, devices * 4), BF16),
-            pltpu.VMEM((128, 2 * width + 128), BF16),
+            pltpu.VMEM((128, 2 * width), BF16),
+            pltpu.VMEM((width, 4 * width), BF16),
             pltpu.VMEM((8, width), F32),
             pltpu.VMEM((8, 128), F32),
             pltpu.VMEM((8, width), F32),
             pltpu.VMEM((8, width), F32),
+            pltpu.VMEM((rows, width), F32),
             pltpu.SemaphoreType.DMA,
             pltpu.SemaphoreType.DMA,
             pltpu.SemaphoreType.DMA((groups,)),
             pltpu.SemaphoreType.DMA,
-            pltpu.SemaphoreType.DMA,
+            pltpu.SemaphoreType.DMA((groups,)),
             pltpu.SemaphoreType.DMA((2,)),
         ],
         compiler_params=pltpu.CompilerParams(

time: 49.2 us -> 40.4 us (0.82)
  Pallas kernels: 45.2 us -> 36.4 us
    pallas_call x1, Pallas kernels: 45.2 us -> 36.4 us  [body(): pl.pallas_call(functools.partial(kernel, n_ing, n_own, G), out_shape=(jax...]
where the time goes in v2:
time: 40.4 us; the launch traced here: 40.2 us
  Pallas kernels  36.4 us (90%)
  local copies, waits for them, and re-layouts  3.13 us (8%)
  between operations  0.64 us (2%)
    pallas_call x1, Pallas kernels, body(): pl.pallas_call(functools.partial(kernel, n_ing, n_own, G), out_shape=(jax...  36.4 us
    unnamed x2, local copies, waits for them, and re-layouts  3.13 us

profile of v2, /device:TPU:1, one launch (start us, length us, event | category | flops | bytes accessed | tf_op | source)
XLA Modules:
  0.0 40.2 jit_solution(6828485030688893816)
XLA Ops:
  0.6 36.4 %scorer.1 = (bf16[1024,256]{1,0:T(8,128)(2,1)}, bf16[6,256]{1,0:T(8,128)(2,1)}) custom-call(s32[1,1024]{1,0:T(1,128)} %bitcast.4, s32[1,1024]{1,0:T(1,128)} %bitcast.5, s32[512]{0:T(512)} %lens_ref.1, s32[128]{0:T(128)} %mig_ref.1, bf16[4,256]{1,0:T(4,128)(2,1)} %conv_ref.1, bf16[48,1024]{1,0:T(8,128)(2,1)} %bitcast.3, bf16[4,2,512,256]{3,2,1,0:T(8,128)(2,1)} %kv_ref.1, ...), custom_call_target="tpu_custom_call" | custom-call | tf_op jit(solution)/shard_map/scorer/pallas_call | solution.py:460
  37.1 1.9 %copy.15 = bf16[1024,256]{1,0:T(8,128)(2,1)} copy(bf16[1024,256]{1,0:T(8,128)(2,1)} %get-tuple-element.4) | data formatting | bytes 1048576
  39.0 1.3 %copy.16 = bf16[6,256]{1,0:T(8,128)(2,1)} copy(bf16[6,256]{1,0:T(8,128)(2,1)} %get-tuple-element.5) | data formatting | bytes 6144

commit v3 on v2

--- a/solution.py
+++ b/solution.py
@@ -9,6 +9,7 @@
 
 HEADS = 4
 MIG = 2
+LOG2E = 1.4426950408889634
 MESH = pl.DeviceIdType.MESH
 F32 = jnp.float32
 BF16 = jnp.bfloat16
@@ -31,19 +32,29 @@
     n_ing,
     n_own,
     G,
+    dev_hbm,
+    slot_hbm,
+    lens_hbm,
+    mig_hbm,
+    conv_hbm,
+    mel_hbm,
+    kv_ref,
+    w_in_hbm,
+    w_state_hbm,
+    w_qkv_hbm,
+    w_out_hbm,
+    out_ref,
+    new_ref,
     dev_ref,
     slot_ref,
     lens_ref,
     mig_ref,
     conv_ref,
     mel_ref,
-    kv_ref,
     w_in_ref,
     w_state_ref,
     w_qkv_ref,
     w_out_ref,
-    out_ref,
-    new_ref,
     snd,
     rcv,
     rsnd,
@@ -61,12 +72,17 @@
     upd_out,
     upd_in,
     acc,
+    marks,
+    lanes,
+    hid,
+    qkvs,
     kv_sem,
     ssem,
     rsem,
     bsem,
     csem,
     usem,
+    in_sem,
 ):
     devices = n_ing * n_own
     groups = devices // G
@@ -79,13 +95,14 @@
     me = ing * n_own + own
 
     N = n_ing
-    yy, zz, core = own // (2 * N), (own // 2) % N, own % 2
-    mine_k = (ing + yy + zz) % N
+    rem = lax.rem
+    yy, zz, core = lax.div(own, 2 * N), rem(lax.div(own, 2), N), rem(own, 2)
+    mine_k = rem(ing + yy + zz, N)
     place = mine_k * G + ing * (2 * N) + yy * 2 + core
 
     def peer(k, dx, dy, dc):
-        x, y, c = (ing + dx) % N, (yy + dy) % N, (core + dc) % 2
-        z = (k + 2 * N - x - y) % N
+        x, y, c = rem(ing + dx, N), rem(yy + dy, N), rem(core + dc, 2)
+        z = rem(k + 2 * N - x - y, N)
         return k * G + x * (2 * N) + y * 2 + c, (x, y * (2 * N) + z * 2 + c)
 
     def each_peer(j, k, start):
@@ -99,11 +116,24 @@
         lax.fori_loop(0, N, step, 0)
         for dx in range(1, N):
             start(*peer(k, dx, 0, 0))
-
-        @pl.when(j > 0)
-        def _():
+        if j > 0:
             start(*peer(k, 0, 0, 0))
 
+    pairs = [
+        (dev_hbm, dev_ref),
+        (slot_hbm, slot_ref),
+        (mel_hbm, mel_ref),
+        (lens_hbm, lens_ref),
+        (conv_hbm, conv_ref),
+        (w_state_hbm, w_state_ref),
+        (w_in_hbm, w_in_ref),
+        (w_qkv_hbm, w_qkv_ref),
+        (w_out_hbm, w_out_ref),
+        (mig_hbm, mig_ref),
+    ]
+    loads = [pltpu.make_async_copy(a, b, in_sem.at[i]) for i, (a, b) in enumerate(pairs)]
+    for load in loads:
+        load.start()
     kv_copy = pltpu.make_async_copy(kv_ref, kvb, kv_sem)
     kv_copy.start()
 
@@ -121,6 +151,8 @@
         x = lax.rem(ing + a, n_ing)
         pl.semaphore_signal(barrier, inc=1, device_id=(x, own), device_id_type=MESH)
 
+    for load in loads[:3]:
+        load.wait()
     dev = dev_ref[...]
     slot = slot_ref[...]
     step = 256
@@ -145,8 +177,6 @@
     half = jnp.concatenate([mel_ref[...], slots], axis=0)
     mel2[...] = jnp.concatenate([half, half], axis=0).T
 
-    pl.semaphore_wait(barrier, devices - 1)
-
     tile = G * 8
     low = iota((tile, 128), 1) < 64
     lines = jnp.concatenate([iota((tile, 128), 0).astype(F32).astype(BF16)] * (rows // 128), axis=1)
@@ -167,8 +197,7 @@
             device_id_type=MESH,
         ).start()
 
-    def pack(j, c):
-        g = (mine_k + j) % groups
+    for g in range(groups):
         picks = jnp.concatenate(
             [
                 jnp.where(lines == spread(code0, g), one, zero),
@@ -178,14 +207,15 @@
         )
         both = mm(picks, mel2[...])
         packed = jnp.where(low, both[:tile], both[tile:]).astype(BF16)
-        snd[pl.ds(g * G, G)] = packed.reshape(G, 8, 128)
-
-        each_peer(j, g, send)
-        return c
-
-    lax.fori_loop(0, groups, pack, 0)
+        snd[g * G : g * G + G] = packed.reshape(G, 8, 128)
+
+    pl.semaphore_wait(barrier, devices - 1)
+    for j in range(groups):
+        each_peer(j, rem(mine_k + j, groups), send)
     rcv[pl.ds(place, 1)] = snd[pl.ds(place, 1)]
 
+    for load in loads[3:]:
+        load.wait()
     r4 = iota((16, width), 0)
     states = mm(conv_ref[...], w_state_ref[...])
     tiled = jnp.zeros((16, width), F32)
@@ -246,19 +276,6 @@
                     vc[2 * pair, :, there] = even
                     vc[2 * pair + 1, :, there] = odd
 
-    diag = iota((128, 128), 0) == iota((128, 128), 1)
-    for b in range(rows // 128):
-        here = slice(b * 128, b * 128 + 128)
-        c0 = jnp.sum(jnp.where(diag, code0[:, here].astype(F32), 0.0), axis=1, keepdims=True)
-        c2 = jnp.sum(jnp.where(diag, code2[:, here].astype(F32), 0.0), axis=1, keepdims=True)
-        across = iota((128, 256), 1).astype(F32).astype(BF16)
-        for t in range(devices * 8 // 256):
-            near = jnp.broadcast_to(c0 - t * 256, (128, 256)).astype(BF16)
-            um[here, t * 256 : t * 256 + 256] = jnp.where(across == near, one, zero)
-        for t in range(devices * 4 // 256):
-            near = jnp.broadcast_to(c2 - t * 256, (128, 256)).astype(BF16)
-            ue[here, t * 256 : t * 256 + 256] = jnp.where(across == near, one, zero)
-
     total = 12 * G
     sums[...] = jnp.zeros_like(sums)
     counts[...] = jnp.zeros_like(counts)
@@ -270,29 +287,30 @@
     low_r = iota((total, 128), 1) < 64
     sub = iota((G // 2, 8, 128), 1) < 4
 
-    def score(j, c):
-        g = (mine_k + groups - j) % groups
-
-        @pl.when(j == 0)
-        def _():
-            part = rcv.at[pl.ds(g * G, G - 1)]
-            pltpu.make_async_copy(part, part, rsem.at[g]).wait()
-
-        @pl.when(j > 0)
-        def _():
-            part = rcv.at[pl.ds(g * G, G)]
-            pltpu.make_async_copy(part, part, rsem.at[g]).wait()
-
+    def front(j):
+        g = rem(mine_k + groups - j, groups)
+        part = rcv.at[pl.ds(g * G, G if j else G - 1)]
+        pltpu.make_async_copy(part, part, rsem.at[g]).wait()
         a = rcv[pl.ds(g * G, G)].reshape(8 * G, 128)
         x = pltpu.roll(mm(pick, a), 64, 1).astype(BF16)
         both = jnp.concatenate([a, x], axis=0)
         f = mm(both, wx[...])
         pre = f[:, :width]
-        in_lanes = f[:, width : 2 * width]
+        hidden = (pre * jax.nn.sigmoid(pre)).astype(BF16)
+        marks[j % 2] = both
+        lanes[j % 2] = f[:, width:]
+        hid[j % 2] = hidden
+        qkv = mm(hidden, wq[...])
+        qkvs[j % 2, :, : 2 * width] = qkv[:, : 2 * width] * LOG2E
+        qkvs[j % 2, :, 2 * width :] = qkv[:, 2 * width :]
+
+    def heads(j):
+        g = rem(mine_k + groups - j, groups)
+        qkv = qkvs.at[j % 2]
+        in_lanes = lanes[j % 2]
         mask4 = in_lanes.astype(BF16)
-        spare = in_lanes * past
-        hidden = (pre * jax.nn.sigmoid(pre)).astype(BF16)
-        qkv = mm(hidden, wq[...])
+        kept = 1.0 - in_lanes * past
+        hidden = hid[j % 2]
         outs = []
         for pair in range(HEADS // 2):
             kcol = 2 * width + pair * 128
@@ -306,9 +324,10 @@
                 wide = jnp.concatenate([q, q], axis=1) * mask4
                 s = mm(wide, kt[2 * pair + h])
                 top = jnp.max(s, axis=1, keepdims=True)
-                e = jnp.exp(s - top)
-                part = (e[:, :128] + e[:, 128:256]) + (e[:, 256:384] + e[:, 384:])
-                part = part - spare[:, :128] * e[:, :128] - spare[:, 128:] * e[:, 128:256]
+                e = jnp.exp2(s - top)
+                part = (e[:, :128] * kept[:, :128] + e[:, 128:256] * kept[:, 128:]) + (
+                    e[:, 256:384] + e[:, 384:]
+                )
                 totals.append(jnp.sum(part, axis=1, keepdims=True))
                 tops.append(top)
                 o = mm(e.astype(BF16), vc[2 * pair + h])
@@ -323,8 +342,8 @@
             own1 = jnp.sum(jnp.where(low_r, 0.0, prod), axis=1, keepdims=True)
             mine = jnp.where(low_r, own0, own1)
             peak = jnp.maximum(top, mine)
-            ea = jnp.exp(top - peak)
-            eb = jnp.exp(mine - peak)
+            ea = jnp.exp2(top - peak)
+            eb = jnp.exp2(mine - peak)
             outs.append(((ea * mix + eb * v) / (ea * tot + eb)).astype(BF16))
         attn = jnp.concatenate(outs, axis=1)
         scored = (hidden.astype(F32) + mm(attn, w_out_ref[...])).astype(BF16)
@@ -349,15 +368,31 @@
             ).start()
 
         each_peer(j, g, back)
-        marks = lax.dot_general(
-            slot_lane, both, (((1,), (1,)), ((), ())), preferred_element_type=F32
+        hits = lax.dot_general(
+            slot_lane, marks[j % 2], (((1,), (1,)), ((), ())), preferred_element_type=F32
         )
-        sums[...] += mm(marks.astype(BF16), scored)
-        counts[...] += jnp.sum(marks, axis=1, keepdims=True)
-        return c
-
-    lax.fori_loop(0, groups, score, 0)
+        sums[...] += mm(hits.astype(BF16), scored)
+        counts[...] += jnp.sum(hits, axis=1, keepdims=True)
+
+    front(0)
+    for j in range(groups):
+        if j + 1 < groups:
+            front(j + 1)
+        heads(j)
     ret[pl.ds(place, 1)] = rsnd[pl.ds(place, 1)]
+
+    diag = iota((128, 128), 0) == iota((128, 128), 1)
+    for b in range(rows // 128):
+        here = slice(b * 128, b * 128 + 128)
+        c0 = jnp.sum(jnp.where(diag, code0[:, here].astype(F32), 0.0), axis=1, keepdims=True)
+        c2 = jnp.sum(jnp.where(diag, code2[:, here].astype(F32), 0.0), axis=1, keepdims=True)
+        across = iota((128, 256), 1).astype(F32).astype(BF16)
+        for t in range(devices * 8 // 256):
+            near = jnp.broadcast_to(c0 - t * 256, (128, 256)).astype(BF16)
+            um[here, t * 256 : t * 256 + 256] = jnp.where(across == near, one, zero)
+        for t in range(devices * 4 // 256):
+            near = jnp.broadcast_to(c2 - t * 256, (128, 256)).astype(BF16)
+            ue[here, t * 256 : t * 256 + 256] = jnp.where(across == near, one, zero)
 
     n = counts[0:sess, 0:1]
     mean = sums[0:sess, :] / jnp.maximum(n, 1.0)
@@ -456,28 +491,25 @@
     G = n_own
     groups = devices // G
     vmem = pl.BlockSpec(memory_space=pltpu.VMEM)
-    smem = pl.BlockSpec(memory_space=pltpu.SMEM)
     return pl.pallas_call(
         functools.partial(kernel, n_ing, n_own, G),
         out_shape=(
             jax.ShapeDtypeStruct((rows, width), BF16),
             jax.ShapeDtypeStruct((sess + MIG, width), BF16),
         ),
-        in_specs=[
-            vmem,
-            vmem,
-            smem,
-            smem,
-            vmem,
-            vmem,
-            pl.BlockSpec(memory_space=pl.ANY),
-            vmem,
-            vmem,
-            vmem,
-            vmem,
-        ],
+        in_specs=[pl.BlockSpec(memory_space=pltpu.HBM)] * 11,
         out_specs=(vmem, vmem),
         scratch_shapes=[
+            pltpu.VMEM((1, rows), I32),
+            pltpu.VMEM((1, rows), I32),
+            pltpu.SMEM(window_length.shape, I32),
+            pltpu.SMEM(migrate_count.shape, I32),
+            pltpu.VMEM(conv_state.shape, BF16),
+            pltpu.VMEM((mel, rows), BF16),
+            pltpu.VMEM(w_in.shape, BF16),
+            pltpu.VMEM(w_state.shape, BF16),
+            pltpu.VMEM(w_qkv.shape, BF16),
+            pltpu.VMEM(w_out.shape, BF16),
             pltpu.VMEM((devices, 8, 128), BF16),
             pltpu.VMEM((devices, 8, 128), BF16),
             pltpu.VMEM((devices, 24, 128), BF16),
@@ -495,29 +527,39 @@
             pltpu.VMEM((8, width), F32),
             pltpu.VMEM((8, width), F32),
             pltpu.VMEM((rows, width), F32),
+            pltpu.VMEM((2, 12 * G, 128), BF16),
+            pltpu.VMEM((2, 12 * G, width), F32),
+            pltpu.VMEM((2, 12 * G, width), BF16),
+            pltpu.VMEM((2, 12 * G, 4 * width), F32),
             pltpu.SemaphoreType.DMA,
             pltpu.SemaphoreType.DMA,
             pltpu.SemaphoreType.DMA((groups,)),
             pltpu.SemaphoreType.DMA,
             pltpu.SemaphoreType.DMA((groups,)),
             pltpu.SemaphoreType.DMA((2,)),
+            pltpu.SemaphoreType.DMA((10,)),
         ],
         compiler_params=pltpu.CompilerParams(
-            collective_id=0, has_side_effects=True, vmem_limit_bytes=56 << 20
+            collective_id=0, has_side_effects=True, vmem_limit_bytes=40 << 20
         ),
         name="scorer",
     )(
-        row_device.reshape(1, rows),
-        row_slot.reshape(1, rows),
-        window_length,
-        migrate_count,
-        conv_state,
-        frame_mel.T,
-        kv_cache,
-        w_in,
-        w_state,
-        w_qkv,
-        w_out,
+        *(
+            pltpu.with_memory_space_constraint(a, pltpu.HBM)
+            for a in (
+                row_device.reshape(1, rows),
+                row_slot.reshape(1, rows),
+                window_length,
+                migrate_count,
+                conv_state,
+                frame_mel.T,
+                kv_cache,
+                w_in,
+                w_state,
+                w_qkv,
+                w_out,
+            )
+        )
     )
 
 

time: 40.4 us -> 36.3 us (0.90)
  Pallas kernels: 36.4 us -> 34.1 us
  local copies, waits for them, and re-layouts: 3.13 us -> 1.39 us
    pallas_call x1, Pallas kernels: 36.4 us -> 34.1 us  [body(): pl.pallas_call(functools.partial(kernel, n_ing, n_own, G), out_shape=(jax...]
    unnamed x2, local copies, waits for them, and re-layouts: 3.13 us -> 1.39 us
where the time goes in v3:
time: 36.3 us; the launch traced here: 36.2 us
  Pallas kernels  34.1 us (94%)
  local copies, waits for them, and re-layouts  1.39 us (4%)
  between operations  0.64 us (2%)
    pallas_call x1, Pallas kernels, body(): pl.pallas_call(functools.partial(kernel, n_ing, n_own, G), out_shape=(jax...  34.1 us
    unnamed x2, local copies, waits for them, and re-layouts  1.39 us

profile of v3, /device:TPU:1, one launch (start us, length us, event | category | flops | bytes accessed | tf_op | source)
XLA Modules:
  0.0 36.2 jit_solution(11559093741464393116)
XLA Ops:
  0.6 34.1 %scorer.1 = (bf16[1024,256]{1,0:T(8,128)(2,1)S(1)}, bf16[6,256]{1,0:T(8,128)(2,1)S(1)}) custom-call(s32[1,1024]{1,0:T(1,128)} %bitcast.4, s32[1,1024]{1,0:T(1,128)} %bitcast.5, s32[512]{0:T(512)} %lens_hbm.1, s32[128]{0:T(128)} %mig_hbm.1, bf16[4,256]{1,0:T(4,128)(2,1)} %conv_hbm.1, bf16[48,1024]{1,0:T(8,128)(2,1)} %bitcast.3, ...), custom_call_target="tpu_custom_call" | custom-call | tf_op jit(solution)/shard_map/scorer/pallas_call | solution.py:494
  34.8 0.8 %copy.15 = bf16[1024,256]{1,0:T(8,128)(2,1)} copy(bf16[1024,256]{1,0:T(8,128)(2,1)S(1)} %get-tuple-element.4) | data formatting | bytes 1048576
  35.6 0.6 %copy.16 = bf16[6,256]{1,0:T(8,128)(2,1)} copy(bf16[6,256]{1,0:T(8,128)(2,1)S(1)} %get-tuple-element.5) | data formatting | bytes 6144

commit v4 on v3

--- a/solution.py
+++ b/solution.py
@@ -73,7 +73,11 @@
     upd_in,
     acc,
     marks,
+    raw,
+    expo,
     lanes,
+    masks,
+    kept,
     hid,
     qkvs,
     kv_sem,
@@ -287,10 +291,13 @@
     low_r = iota((total, 128), 1) < 64
     sub = iota((G // 2, 8, 128), 1) < 4
 
-    def front(j):
+    def arrive(j):
         g = rem(mine_k + groups - j, groups)
         part = rcv.at[pl.ds(g * G, G if j else G - 1)]
         pltpu.make_async_copy(part, part, rsem.at[g]).wait()
+
+    def front(j):
+        g = rem(mine_k + groups - j, groups)
         a = rcv[pl.ds(g * G, G)].reshape(8 * G, 128)
         x = pltpu.roll(mm(pick, a), 64, 1).astype(BF16)
         both = jnp.concatenate([a, x], axis=0)
@@ -299,6 +306,8 @@
         hidden = (pre * jax.nn.sigmoid(pre)).astype(BF16)
         marks[j % 2] = both
         lanes[j % 2] = f[:, width:]
+        masks[j % 2] = f[:, width:].astype(BF16)
+        kept[j % 2] = 1.0 - f[:, width:] * past
         hid[j % 2] = hidden
         qkv = mm(hidden, wq[...])
         qkvs[j % 2, :, : 2 * width] = qkv[:, : 2 * width] * LOG2E
@@ -307,10 +316,7 @@
     def heads(j):
         g = rem(mine_k + groups - j, groups)
         qkv = qkvs.at[j % 2]
-        in_lanes = lanes[j % 2]
-        mask4 = in_lanes.astype(BF16)
-        kept = 1.0 - in_lanes * past
-        hidden = hid[j % 2]
+        b = j % 2
         outs = []
         for pair in range(HEADS // 2):
             kcol = 2 * width + pair * 128
@@ -321,17 +327,18 @@
                 at = pair * 256 + h * 128
                 qs.append(qkv[:, at : at + 128])
                 q = qs[h].astype(BF16)
-                wide = jnp.concatenate([q, q], axis=1) * mask4
-                s = mm(wide, kt[2 * pair + h])
-                top = jnp.max(s, axis=1, keepdims=True)
-                e = jnp.exp2(s - top)
-                part = (e[:, :128] * kept[:, :128] + e[:, 128:256] * kept[:, 128:]) + (
+                wide = jnp.concatenate([q, q], axis=1) * masks[b]
+                raw[h] = mm(wide, kt[2 * pair + h])
+                top = jnp.max(raw[h], axis=1, keepdims=True)
+                e = jnp.exp2(raw[h] - top)
+                expo[h] = e.astype(BF16)
+                part = (e[:, :128] * kept[b, :, :128] + e[:, 128:256] * kept[b, :, 128:]) + (
                     e[:, 256:384] + e[:, 384:]
                 )
                 totals.append(jnp.sum(part, axis=1, keepdims=True))
                 tops.append(top)
-                o = mm(e.astype(BF16), vc[2 * pair + h])
-                mixed.append(o[:, :128] * in_lanes[:, :128] + o[:, 128:] * in_lanes[:, 128:])
+                o = mm(expo[h], vc[2 * pair + h])
+                mixed.append(o[:, :128] * lanes[b, :, :128] + o[:, 128:] * lanes[b, :, 128:])
             mix = jnp.where(low_r, mixed[0], mixed[1]) + pltpu.roll(
                 jnp.where(low_r, mixed[1], mixed[0]), 64, 1
             )
@@ -345,8 +352,10 @@
             ea = jnp.exp2(top - peak)
             eb = jnp.exp2(mine - peak)
             outs.append(((ea * mix + eb * v) / (ea * tot + eb)).astype(BF16))
+        if j + 1 < groups:
+            front(j + 1)
         attn = jnp.concatenate(outs, axis=1)
-        scored = (hidden.astype(F32) + mm(attn, w_out_ref[...])).astype(BF16)
+        scored = (hid[b].astype(F32) + mm(attn, w_out_ref[...])).astype(BF16)
         wide = scored.astype(F32)
         first = pl.ds(g * G, G)
         rsnd[first, 0:8, :] = scored[: 8 * G, :128].reshape(G, 8, 128)
@@ -374,10 +383,11 @@
         sums[...] += mm(hits.astype(BF16), scored)
         counts[...] += jnp.sum(hits, axis=1, keepdims=True)
 
+    arrive(0)
     front(0)
     for j in range(groups):
         if j + 1 < groups:
-            front(j + 1)
+            arrive(j + 1)
         heads(j)
     ret[pl.ds(place, 1)] = rsnd[pl.ds(place, 1)]
 
@@ -528,6 +538,10 @@
             pltpu.VMEM((8, width), F32),
             pltpu.VMEM((rows, width), F32),
             pltpu.VMEM((2, 12 * G, 128), BF16),
+            pltpu.VMEM((2, 12 * G, window), F32),
+            pltpu.VMEM((2, 12 * G, window), BF16),
+            pltpu.VMEM((2, 12 * G, width), F32),
+            pltpu.VMEM((2, 12 * G, width), BF16),
             pltpu.VMEM((2, 12 * G, width), F32),
             pltpu.VMEM((2, 12 * G, width), BF16),
             pltpu.VMEM((2, 12 * G, 4 * width), F32),

time: 36.3 us -> 35.5 us (0.978)
  Pallas kernels: 34.1 us -> 33.4 us
    pallas_call x1, Pallas kernels: 34.1 us -> 33.4 us  [body(): pl.pallas_call(functools.partial(kernel, n_ing, n_own, G), out_shape=(jax...]
where the time goes in v4:
time: 35.5 us; the launch traced here: 35.4 us
  Pallas kernels  33.4 us (94%)
  local copies, waits for them, and re-layouts  1.39 us (4%)
  between operations  0.64 us (2%)
    pallas_call x1, Pallas kernels, body(): pl.pallas_call(functools.partial(kernel, n_ing, n_own, G), out_shape=(jax...  33.4 us
    unnamed x2, local copies, waits for them, and re-layouts  1.39 us

profile of v4, /device:TPU:1, one launch (start us, length us, event | category | flops | bytes accessed | tf_op | source)
XLA Modules:
  0.0 35.4 jit_solution(14624646358696736233)
XLA Ops:
  0.6 33.4 %scorer.1 = (bf16[1024,256]{1,0:T(8,128)(2,1)S(1)}, bf16[6,256]{1,0:T(8,128)(2,1)S(1)}) custom-call(s32[1,1024]{1,0:T(1,128)} %bitcast.4, s32[1,1024]{1,0:T(1,128)} %bitcast.5, s32[512]{0:T(512)} %lens_hbm.1, s32[128]{0:T(128)} %mig_hbm.1, bf16[4,256]{1,0:T(4,128)(2,1)} %conv_hbm.1, bf16[48,1024]{1,0:T(8,128)(2,1)} %bitcast.3, ...), custom_call_target="tpu_custom_call" | custom-call | tf_op jit(solution)/shard_map/scorer/pallas_call | solution.py:504
  34.0 0.8 %copy.15 = bf16[1024,256]{1,0:T(8,128)(2,1)} copy(bf16[1024,256]{1,0:T(8,128)(2,1)S(1)} %get-tuple-element.4) | data formatting | bytes 1048576
  34.8 0.6 %copy.16 = bf16[6,256]{1,0:T(8,128)(2,1)} copy(bf16[6,256]{1,0:T(8,128)(2,1)S(1)} %get-tuple-element.5) | data formatting | bytes 6144

commit v5 on v4

--- a/solution.py
+++ b/solution.py
@@ -201,7 +201,8 @@
             device_id_type=MESH,
         ).start()
 
-    for g in range(groups):
+    def pack(j):
+        g = rem(mine_k + j, groups)
         picks = jnp.concatenate(
             [
                 jnp.where(lines == spread(code0, g), one, zero),
@@ -211,10 +212,15 @@
         )
         both = mm(picks, mel2[...])
         packed = jnp.where(low, both[:tile], both[tile:]).astype(BF16)
-        snd[g * G : g * G + G] = packed.reshape(G, 8, 128)
-
+        snd[pl.ds(g * G, G)] = packed.reshape(G, 8, 128)
+
+    pack(0)
+    pack(1)
     pl.semaphore_wait(barrier, devices - 1)
-    for j in range(groups):
+    each_peer(0, mine_k, send)
+    each_peer(1, rem(mine_k + 1, groups), send)
+    for j in range(2, groups):
+        pack(j)
         each_peer(j, rem(mine_k + j, groups), send)
     rcv[pl.ds(place, 1)] = snd[pl.ds(place, 1)]
 

time: 35.5 us -> 35.3 us (level)
  no operation moved by 1% of the time
where the time goes in v5:
time: 35.3 us; the launch traced here: 35.1 us
  Pallas kernels  33.1 us (94%)
  local copies, waits for them, and re-layouts  1.39 us (4%)
  between operations  0.64 us (2%)
    pallas_call x1, Pallas kernels, body(): pl.pallas_call(functools.partial(kernel, n_ing, n_own, G), out_shape=(jax...  33.1 us
    unnamed x2, local copies, waits for them, and re-layouts  1.39 us

profile of v5, /device:TPU:1, one launch (start us, length us, event | category | flops | bytes accessed | tf_op | source)
XLA Modules:
  0.0 35.1 jit_solution(5244898251509275141)
XLA Ops:
  0.6 33.1 %scorer.1 = (bf16[1024,256]{1,0:T(8,128)(2,1)S(1)}, bf16[6,256]{1,0:T(8,128)(2,1)S(1)}) custom-call(s32[1,1024]{1,0:T(1,128)} %bitcast.4, s32[1,1024]{1,0:T(1,128)} %bitcast.5, s32[512]{0:T(512)} %lens_hbm.1, s32[128]{0:T(128)} %mig_hbm.1, bf16[4,256]{1,0:T(4,128)(2,1)} %conv_hbm.1, bf16[48,1024]{1,0:T(8,128)(2,1)} %bitcast.3, ...), custom_call_target="tpu_custom_call" | custom-call | tf_op jit(solution)/shard_map/scorer/pallas_call | solution.py:510
  33.8 0.8 %copy.15 = bf16[1024,256]{1,0:T(8,128)(2,1)} copy(bf16[1024,256]{1,0:T(8,128)(2,1)S(1)} %get-tuple-element.4) | data formatting | bytes 1048576
  34.6 0.6 %copy.16 = bf16[6,256]{1,0:T(8,128)(2,1)} copy(bf16[6,256]{1,0:T(8,128)(2,1)S(1)} %get-tuple-element.5) | data formatting | bytes 6144
